TPU v7x, 32 devices: a whole 2x2x4 slice. The times are simulated.
32 devices in a mesh: rep: 2 (over x), seq: 16 (over z, y, core).
Axes of the slice: x: 2, y: 2, z: 4, core: 2. Of those that a mesh axis runs over, the one named last changes fastest.
Arguments:
- keys: bfloat16 [2048, 5120], P(('rep', 'seq')), parts along dimension 0, may hold values from -36 to 36
- values: bfloat16 [2048, 5120], P(('rep', 'seq')), parts along dimension 0, may hold values from -6 to 6
- queries: bfloat16 [2, 1024, 5120], P(None, ('rep', 'seq')), parts along dimension 1, may hold values from -6 to 6
Outputs:
- attended: bfloat16 [2, 1024, 5120], P(None, ('rep', 'seq')), parts along dimension 1
There are 2 independent parts, one for each index of `rep`. A program takes and returns all parts, laid end to end along the dimension named above; each array names one. Nothing has to cross between parts.
All inputs are finite; a program needn't handle non-finite values.
Results may differ from a plain program's by a relative error of at most 0.0038.
Values may be sent and summed in bfloat16 or wider, within the bound.
A program may use at most 128 MiB of HBM per device.

v0:
```python
import math

import jax
import jax.numpy as jnp
from jax import lax
from jax.sharding import PartitionSpec as P

HEAD_DIM = 128
GROUPS = 8


def local(keys, values, queries):
    nseq = lax.axis_size("seq")
    blocks = nseq // GROUPS
    ctx_rows, width = keys.shape
    group_width = width // GROUPS
    heads_group = group_width // HEAD_DIM
    layers, tok_rows, _ = queries.shape
    query_total = tok_rows * nseq
    scale = 1.0 / math.sqrt(HEAD_DIM)

    def arrange(local_block):
        return local_block.reshape(ctx_rows // blocks, nseq, group_width)

    def by_source(array):
        return array.reshape((array.shape[0], blocks, GROUPS) + array.shape[2:])

    moved_keys, moved_values = (
        lax.all_to_all(arrange(keys), "seq", split_axis=1, concat_axis=1, tiled=True),
        lax.all_to_all(arrange(values), "seq", split_axis=1, concat_axis=1, tiled=True),
    )
    moved_keys = moved_keys.reshape(-1, group_width)
    moved_values = moved_values.reshape(-1, group_width)
    layer_outs = []
    for layer in range(layers):
        local_query = queries[layer]
        per_group = local_query.reshape(tok_rows, GROUPS, group_width)
        received = lax.all_to_all(
            jnp.broadcast_to(per_group[:, None], (tok_rows, blocks, GROUPS, group_width)).reshape(
                tok_rows, nseq, group_width
            ),
            "seq",
            split_axis=1,
            concat_axis=0,
            tiled=True,
        )
        own_block = received.reshape(query_total, group_width)

        def one_head(head):
            start = head * HEAD_DIM
            q_head = lax.dynamic_slice_in_dim(own_block, start, HEAD_DIM, 1)
            k_head = lax.dynamic_slice_in_dim(moved_keys, start, HEAD_DIM, 1)
            v_head = lax.dynamic_slice_in_dim(moved_values, start, HEAD_DIM, 1)
            scores = (
                lax.dot_general(
                    q_head, k_head, (((1,), (1,)), ((), ())), preferred_element_type=jnp.float32
                )
                * scale
            )
            peak = jnp.max(scores, axis=1)
            expo = jnp.exp(scores - peak[:, None])
            total = jnp.sum(expo, axis=1)
            summed = jnp.dot(expo.astype(jnp.bfloat16), v_head, preferred_element_type=jnp.float32)
            return (summed, peak, total)

        summed, peak, total = lax.map(one_head, jnp.arange(heads_group, dtype=jnp.int32))
        shaped = (
            summed.reshape(heads_group, nseq, tok_rows, HEAD_DIM),
            peak.reshape(heads_group, nseq, tok_rows),
            total.reshape(heads_group, nseq, tok_rows),
        )
        combine_summed = lax.all_to_all(shaped[0], "seq", split_axis=1, concat_axis=1, tiled=True)
        combine_peak = lax.all_to_all(shaped[1], "seq", split_axis=1, concat_axis=1, tiled=True)
        combine_total = lax.all_to_all(shaped[2], "seq", split_axis=1, concat_axis=1, tiled=True)
        rows = combine_peak.shape[2]
        summed_s = by_source(combine_summed)
        peak_s = by_source(combine_peak)
        total_s = by_source(combine_total)
        highest = jnp.max(peak_s, axis=1)
        factor = jnp.exp(peak_s - highest[:, None])
        denom = jnp.sum(factor * total_s, axis=1)
        numer = jnp.sum(factor[..., None] * summed_s, axis=1)
        result = numer / denom[..., None]
        result = jnp.transpose(result, (2, 1, 0, 3)).reshape(rows, GROUPS * heads_group * HEAD_DIM)
        mixed = result.astype(jnp.bfloat16)
        layer_outs.append(mixed)
    return jnp.stack(layer_outs)


def solution(mesh):
    return jax.shard_map(
        local,
        mesh=mesh,
        in_specs=(P(("rep", "seq"), None), P(("rep", "seq"), None), P(None, ("rep", "seq"), None)),
        out_specs=P(None, ("rep", "seq"), None),
        check_vma=False,
    )
```

profile of v0, /device:TPU:0, one launch (start us, length us, event | category | flops | bytes accessed | tf_op | source)
XLA Modules:
  0.0 212.0 jit_solution(11663222374262786308)
XLA Ops:
  0.0 1.4 reshape.112
  1.4 1.0 copy.39
  2.4 7.4 %all-to-all-start.1 = ((bf16[32,16,640]{2,0,1:T(8,128)(2,1)}), bf16[32,16,640]{2,0,1:T(8,128)(2,1)S(1)}, u32[]{:S(2)}, u32[]{:S(2)}) async-start(bf16[32,16,640]{2,0,1:T(8,128)(2,1)} %copy.39), calls=%async_computation.1 | async-start | bytes 1310720 | tf_op jit(solution)/shard_map/all_to_all | solution.py:29
  10.1 1.0 copy.41
  11.1 15.3 %all-to-all-done.1 = bf16[32,16,640]{2,0,1:T(8,128)(2,1)S(1)} async-done(((bf16[32,16,640]{2,0,1:T(8,128)(2,1)}), bf16[32,16,640]{2,0,1:T(8,128)(2,1)S(1)}, u32[]{:S(2)}, u32[]{:S(2)}) %all-to-all-start.1) | async-done | bytes 655392 | tf_op jit(solution)/shard_map/all_to_all | solution.py:29
  26.4 4.7 %all-to-all-start.2 = ((bf16[32,16,640]{2,0,1:T(8,128)(2,1)}), bf16[32,16,640]{2,0,1:T(8,128)(2,1)S(1)}, u32[]{:S(2)}, u32[]{:S(2)}) async-start(bf16[32,16,640]{2,0,1:T(8,128)(2,1)} %copy.41), calls=%async_computation.2 | async-start | bytes 1310720 | tf_op jit(solution)/shard_map/all_to_all | solution.py:30
  31.2 16.4 %all-to-all-done.2 = bf16[32,16,640]{2,0,1:T(8,128)(2,1)S(1)} async-done(((bf16[32,16,640]{2,0,1:T(8,128)(2,1)}), bf16[32,16,640]{2,0,1:T(8,128)(2,1)S(1)}, u32[]{:S(2)}, u32[]{:S(2)}) %all-to-all-start.2) | async-done | bytes 655392 | tf_op jit(solution)/shard_map/all_to_all | solution.py:30
  48.5 4.7 %all-to-all-start = ((bf16[32,16,640]{2,0,1:T(8,128)(2,1)}), bf16[32,16,640]{2,0,1:T(8,128)(2,1)S(1)}, u32[]{:S(2)}, u32[]{:S(2)}) async-start(bf16[32,16,640]{2,0,1:T(8,128)(2,1)} %bitcast.8), calls=%async_computation | async-start | bytes 1310720 | tf_op jit(solution)/shard_map/all_to_all | solution.py:38
  53.7 16.0 %all-to-all-done = bf16[32,16,640]{2,0,1:T(8,128)(2,1)S(1)} async-done(((bf16[32,16,640]{2,0,1:T(8,128)(2,1)}), bf16[32,16,640]{2,0,1:T(8,128)(2,1)S(1)}, u32[]{:S(2)}, u32[]{:S(2)}) %all-to-all-start) | async-done | bytes 655392 | tf_op jit(solution)/shard_map/all_to_all | solution.py:38
  69.8 1.0 broadcast_in_dim.45
  70.7 4.7 %all-to-all-start.6 = ((bf16[32,16,640]{2,0,1:T(8,128)(2,1)}), bf16[32,16,640]{2,0,1:T(8,128)(2,1)S(1)}, u32[]{:S(2)}, u32[]{:S(2)}) async-start(bf16[32,16,640]{2,0,1:T(8,128)(2,1)} %bitcast.20), calls=%async_computation.6 | async-start | bytes 1310720 | tf_op jit(solution)/shard_map/all_to_all | solution.py:38
  75.5 15.8 %while.28 = (s32[]{:T(128)}, f32[5,512,128]{2,1,0:T(8,128)S(1)}, f32[5,512]{1,0:T(8,128)S(1)}, f32[5,512]{1,0:T(8,128)S(1)}, s32[5]{0:T(128)S(1)}, /*index=5*/bf...) while((s32[]{:T(128)}, f32[5,512,128]{2,1,0:T(8,128)S(1)}, ...), condition=%wide.region_3.4_spmd, body=%wide.region_0.3_spmd.sunk | while | flops 135789568 | bytes 3818687 | solution.py:66
  76.8 1.2 fusion.45
  79.9 1.2 fusion.45
  83.1 1.2 fusion.45
  86.3 1.2 fusion.45
  89.4 1.2 fusion.45
  92.4 6.0 %all-to-all-start.3 = ((f32[16,1,160]{2,1,0:T(1,128)}), f32[16,1,160]{2,1,0:T(1,128)S(1)}, u32[]{:S(2)}, u32[]{:S(2)}) async-start(f32[16,1,160]{2,1,0:T(1,128)} %reshape.134), calls=%async_computation.3 | async-start | bytes 32768 | tf_op jit(solution)/shard_map/all_to_all | solution.py:73
  99.2 5.7 %all-to-all-done.3 = f32[16,1,160]{2,1,0:T(1,128)S(1)} async-done(((f32[16,1,160]{2,1,0:T(1,128)}), f32[16,1,160]{2,1,0:T(1,128)S(1)}, u32[]{:S(2)}, u32[]{:S(2)}) %all-to-all-start.3) | async-done | bytes 10272 | tf_op jit(solution)/shard_map/all_to_all | solution.py:73
  104.9 3.5 %all-to-all-start.5 = ((f32[16,1,160]{2,1,0:T(1,128)}), f32[16,1,160]{2,1,0:T(1,128)S(1)}, u32[]{:S(2)}, u32[]{:S(2)}) async-start(f32[16,1,160]{2,1,0:T(1,128)} %reshape.136), calls=%async_computation.5 | async-start | bytes 32768 | tf_op jit(solution)/shard_map/all_to_all | solution.py:74
  108.5 11.4 %while.29 = (s32[]{:T(128)}, f32[5,512,128]{2,1,0:T(8,128)S(1)}, f32[5,512]{1,0:T(8,128)S(1)}, f32[5,512]{1,0:T(8,128)S(1)}, s32[5]{0:T(128)S(1)}, /*index=5*/bf...) while((s32[]{:T(128)}, f32[5,512,128]{2,1,0:T(8,128)S(1)}, ...), condition=%wide.region_10.11_spmd, body=%wide.region_7.10_spmd.sunk | while | flops 135789568 | bytes 3818687 | solution.py:66
  120.1 0.9 reshape.130
  121.0 6.0 %all-to-all-start.7 = ((f32[16,1,160]{2,1,0:T(1,128)}), f32[16,1,160]{2,1,0:T(1,128)S(1)}, u32[]{:S(2)}, u32[]{:S(2)}) async-start(f32[16,1,160]{2,1,0:T(1,128)} %reshape.130), calls=%async_computation.7 | async-start | bytes 32768 | tf_op jit(solution)/shard_map/all_to_all | solution.py:73
  127.8 5.7 %all-to-all-done.7 = f32[16,1,160]{2,1,0:T(1,128)S(1)} async-done(((f32[16,1,160]{2,1,0:T(1,128)}), f32[16,1,160]{2,1,0:T(1,128)S(1)}, u32[]{:S(2)}, u32[]{:S(2)}) %all-to-all-start.7) | async-done | bytes 10272 | tf_op jit(solution)/shard_map/all_to_all | solution.py:73
  133.5 3.5 %all-to-all-start.9 = ((f32[16,1,160]{2,1,0:T(1,128)}), f32[16,1,160]{2,1,0:T(1,128)S(1)}, u32[]{:S(2)}, u32[]{:S(2)}) async-start(f32[16,1,160]{2,1,0:T(1,128)} %reshape.132), calls=%async_computation.9 | async-start | bytes 32768 | tf_op jit(solution)/shard_map/all_to_all | solution.py:74
  137.0 2.5 %copy.46 = f32[5,16,32,128]{3,2,0,1:T(8,128)} copy(f32[5,16,32,128]{3,2,1,0:T(8,128)} %bitcast.89) | data formatting | bytes 2621440 | tf_op jit(solution)/shard_map/reshape | solution.py:68
  139.5 4.0 %all-to-all-done.9 = f32[16,1,160]{2,1,0:T(1,128)S(1)} async-done(((f32[16,1,160]{2,1,0:T(1,128)}), f32[16,1,160]{2,1,0:T(1,128)S(1)}, u32[]{:S(2)}, u32[]{:S(2)}) %all-to-all-start.9) | async-done | bytes 10272 | tf_op jit(solution)/shard_map/all_to_all | solution.py:74
  143.4 3.8 %all-to-all-start.4 = ((f32[5,16,32,128]{3,2,0,1:T(8,128)}), f32[5,16,32,128]{3,2,0,1:T(8,128)S(1)}, u32[]{:S(2)}, u32[]{:S(2)}) async-start(f32[5,16,32,128]{3,2,0,1:T(8,128)} %copy.46), calls=%async_computation.4 | async-start | bytes 2621440 | tf_op jit(solution)/shard_map/all_to_all | solution.py:72
  147.3 1.2 copy.55
  148.4 26.1 %all-to-all-done.4 = f32[5,16,32,128]{3,2,0,1:T(8,128)S(1)} async-done(((f32[5,16,32,128]{3,2,0,1:T(8,128)}), f32[5,16,32,128]{3,2,0,1:T(8,128)S(1)}, u32[]{:S(2)}, u32[]{:S(2)}) %all-to-all-start.4) | async-done | bytes 1310752 | tf_op jit(solution)/shard_map/all_to_all | solution.py:72
  174.5 8.0 %all-to-all-start.8 = ((f32[5,16,32,128]{3,2,0,1:T(8,128)}), f32[5,16,32,128]{3,2,0,1:T(8,128)S(1)}, u32[]{:S(2)}, u32[]{:S(2)}) async-start(f32[5,16,32,128]{3,2,0,1:T(8,128)} %copy.55), calls=%async_computation.8 | async-start | bytes 2621440 | tf_op jit(solution)/shard_map/all_to_all | solution.py:72
  187.5 22.3 %all-to-all-done.8 = f32[5,16,32,128]{3,2,0,1:T(8,128)S(1)} async-done(((f32[5,16,32,128]{3,2,0,1:T(8,128)}), f32[5,16,32,128]{3,2,0,1:T(8,128)S(1)}, u32[]{:S(2)}, u32[]{:S(2)}) %all-to-all-start.8) | async-done | bytes 1310752 | tf_op jit(solution)/shard_map/all_to_all | solution.py:72
  (121 shorter events, 26.1 us)
Async XLA Ops:
  1.4 8.4 %copy-start.4 = (bf16[64,5120]{1,0:T(8,128)(2,1)S(1)}, bf16[64,5120]{1,0:T(8,128)(2,1)}, u32[]{:S(2)}) copy-start(bf16[64,5120]{1,0:T(8,128)(2,1)} %param.8) | copy-start | bytes 1966084
  2.4 24.0 %all-to-all-start.1 = ((bf16[32,16,640]{2,0,1:T(8,128)(2,1)}), bf16[32,16,640]{2,0,1:T(8,128)(2,1)S(1)}, u32[]{:S(2)}, u32[]{:S(2)}) async-start(bf16[32,16,640]{2,0,1:T(8,128)(2,1)} %copy.39), calls=%async_computation.1 | async-start | bytes 1310720 | tf_op jit(solution)/shard_map/all_to_all | solution.py:29
  10.1 20.9 %copy-start.5 = (bf16[2,32,5120]{2,1,0:T(8,128)(2,1)S(1)}, bf16[2,32,5120]{2,1,0:T(8,128)(2,1)}, u32[]{:S(2)}) copy-start(bf16[2,32,5120]{2,1,0:T(8,128)(2,1)} %param.9) | copy-start | bytes 1966084
  26.4 21.3 %all-to-all-start.2 = ((bf16[32,16,640]{2,0,1:T(8,128)(2,1)}), bf16[32,16,640]{2,0,1:T(8,128)(2,1)S(1)}, u32[]{:S(2)}, u32[]{:S(2)}) async-start(bf16[32,16,640]{2,0,1:T(8,128)(2,1)} %copy.41), calls=%async_computation.2 | async-start | bytes 1310720 | tf_op jit(solution)/shard_map/all_to_all | solution.py:30
  48.5 21.3 %all-to-all-start = ((bf16[32,16,640]{2,0,1:T(8,128)(2,1)}), bf16[32,16,640]{2,0,1:T(8,128)(2,1)S(1)}, u32[]{:S(2)}, u32[]{:S(2)}) async-start(bf16[32,16,640]{2,0,1:T(8,128)(2,1)} %bitcast.8), calls=%async_computation | async-start | bytes 1310720 | tf_op jit(solution)/shard_map/all_to_all | solution.py:38
  69.8 5.6 %copy-start.3 = (bf16[32,16,640]{2,0,1:T(8,128)(2,1)}, bf16[32,16,640]{2,0,1:T(8,128)(2,1)S(1)}, u32[]{:S(2)}) copy-start(bf16[32,16,640]{2,0,1:T(8,128)(2,1)S(1)} %all-to-all-done) | copy-start | bytes 1966084
  70.7 21.6 %all-to-all-start.6 = ((bf16[32,16,640]{2,0,1:T(8,128)(2,1)}), bf16[32,16,640]{2,0,1:T(8,128)(2,1)S(1)}, u32[]{:S(2)}, u32[]{:S(2)}) async-start(bf16[32,16,640]{2,0,1:T(8,128)(2,1)} %bitcast.20), calls=%async_computation.6 | async-start | bytes 1310720 | tf_op jit(solution)/shard_map/all_to_all | solution.py:38
  91.3 17.0 %copy-start.2 = (f32[5,512,128]{2,1,0:T(8,128)}, f32[5,512,128]{2,1,0:T(8,128)S(1)}, u32[]{:S(2)}) copy-start(f32[5,512,128]{2,1,0:T(8,128)S(1)} %get-tuple-element.94) | copy-start | bytes 3932164
  92.4 12.5 %all-to-all-start.3 = ((f32[16,1,160]{2,1,0:T(1,128)}), f32[16,1,160]{2,1,0:T(1,128)S(1)}, u32[]{:S(2)}, u32[]{:S(2)}) async-start(f32[16,1,160]{2,1,0:T(1,128)} %reshape.134), calls=%async_computation.3 | async-start | bytes 32768 | tf_op jit(solution)/shard_map/all_to_all | solution.py:73
  104.9 16.1 %all-to-all-start.5 = ((f32[16,1,160]{2,1,0:T(1,128)}), f32[16,1,160]{2,1,0:T(1,128)S(1)}, u32[]{:S(2)}, u32[]{:S(2)}) async-start(f32[16,1,160]{2,1,0:T(1,128)} %reshape.136), calls=%async_computation.5 | async-start | bytes 32768 | tf_op jit(solution)/shard_map/all_to_all | solution.py:74
  120.0 19.5 %copy-start = (f32[5,512,128]{2,1,0:T(8,128)}, f32[5,512,128]{2,1,0:T(8,128)S(1)}, u32[]{:S(2)}) copy-start(f32[5,512,128]{2,1,0:T(8,128)S(1)} %get-tuple-element.97) | copy-start | bytes 3932164
  121.0 12.5 %all-to-all-start.7 = ((f32[16,1,160]{2,1,0:T(1,128)}), f32[16,1,160]{2,1,0:T(1,128)S(1)}, u32[]{:S(2)}, u32[]{:S(2)}) async-start(f32[16,1,160]{2,1,0:T(1,128)} %reshape.130), calls=%async_computation.7 | async-start | bytes 32768 | tf_op jit(solution)/shard_map/all_to_all | solution.py:73
  133.5 10.0 %all-to-all-start.9 = ((f32[16,1,160]{2,1,0:T(1,128)}), f32[16,1,160]{2,1,0:T(1,128)S(1)}, u32[]{:S(2)}, u32[]{:S(2)}) async-start(f32[16,1,160]{2,1,0:T(1,128)} %reshape.132), calls=%async_computation.9 | async-start | bytes 32768 | tf_op jit(solution)/shard_map/all_to_all | solution.py:74
  143.4 3.8 %copy-start.1 = (f32[5,512,128]{2,1,0:T(8,128)S(1)}, f32[5,512,128]{2,1,0:T(8,128)}, u32[]{:S(2)}) copy-start(f32[5,512,128]{2,1,0:T(8,128)} %copy-done) | copy-start | bytes 3932164
  143.4 31.1 %all-to-all-start.4 = ((f32[5,16,32,128]{3,2,0,1:T(8,128)}), f32[5,16,32,128]{3,2,0,1:T(8,128)S(1)}, u32[]{:S(2)}, u32[]{:S(2)}) async-start(f32[5,16,32,128]{3,2,0,1:T(8,128)} %copy.46), calls=%async_computation.4 | async-start | bytes 2621440 | tf_op jit(solution)/shard_map/all_to_all | solution.py:72
  174.5 35.3 %all-to-all-start.8 = ((f32[5,16,32,128]{3,2,0,1:T(8,128)}), f32[5,16,32,128]{3,2,0,1:T(8,128)S(1)}, u32[]{:S(2)}, u32[]{:S(2)}) async-start(f32[5,16,32,128]{3,2,0,1:T(8,128)} %copy.55), calls=%async_computation.8 | async-start | bytes 2621440 | tf_op jit(solution)/shard_map/all_to_all | solution.py:72
where the time goes:
time: 215 us; the launch traced here: 212 us
  waiting for transfers between devices  111 us (52%)
  starting transfers between devices  52.2 us (24%)
  local copies, waits for them, and re-layouts  22.8 us (11%)
  matrix products  11.3 us (5%)
  other arithmetic  6.99 us (3%)
  loops' own time  6.76 us (3%)
    all_to_all x2, waiting for transfers between devices, local(): lax.all_to_all(shaped[0], 'seq', split_axis=1, concat_axis=1, tiled=True)  48.3 us
    all_to_all x1, waiting for transfers between devices, local(): lax.all_to_all(arrange(values), 'seq', split_axis=1, concat_axis=1, tiled...  16.4 us
    all_to_all x2, waiting for transfers between devices, local(): lax.all_to_all(jnp.broadcast_to(per_group[:, None], (tok_rows, blocks, GR...  16.1 us
    all_to_all x1, waiting for transfers between devices, local(): lax.all_to_all(arrange(keys), 'seq', split_axis=1, concat_axis=1, tiled=T...  15.3 us
    all_to_all x2, starting transfers between devices, local(): lax.all_to_all(shaped[1], 'seq', split_axis=1, concat_axis=1, tiled=True)  12 us
    all_to_all x2, starting transfers between devices, local(): lax.all_to_all(shaped[0], 'seq', split_axis=1, concat_axis=1, tiled=True)  11.8 us
    all_to_all x2, waiting for transfers between devices, local(): lax.all_to_all(shaped[1], 'seq', split_axis=1, concat_axis=1, tiled=True)  11.4 us
    all_to_all x2, starting transfers between devices, local(): lax.all_to_all(jnp.broadcast_to(per_group[:, None], (tok_rows, blocks, GR...  9.35 us
  transfers between devices with their start and end apart: 10, of which 8 were waited for; matrix products, arithmetic and copies ran while one was open for 16% of the time, Pallas kernels for 0%

commit v1 on v0

--- a/solution.py
+++ b/solution.py
@@ -1,15 +1,144 @@
+import functools
 import math
 
 import jax
 import jax.numpy as jnp
 from jax import lax
+from jax.experimental import pallas as pl
+from jax.experimental.pallas import tpu as pltpu
 from jax.sharding import PartitionSpec as P
 
 HEAD_DIM = 128
 GROUPS = 8
-
-
-def local(keys, values, queries):
+CORES = 2
+MESH = pl.DeviceIdType.MESH
+ROW_CHUNK = 128
+
+
+def attend_kernel(chips, heads, k_ref, v_ref, q_ref, out_ref, kv, qs, res, kv_send, kv_recv, q_send, q_recv,
+                  fwd_send, fwd_recv, o_send, o_recv):
+    rows = k_ref.shape[0]
+    toks = q_ref.shape[1]
+    group_width = heads * HEAD_DIM
+    half = chips * rows
+    scale = 1.0 / math.sqrt(HEAD_DIM)
+    rep = lax.axis_index("rep")
+    me = lax.axis_index("seq")
+    chip = lax.div(me, CORES)
+    core = lax.rem(me, CORES)
+    partner = me + 1 - 2 * core
+
+    def other(mask):
+        total = 0
+        for bit in range(chips.bit_length() - 1):
+            mine = lax.rem(lax.div(chip, 1 << bit), 2)
+            total = total + ((1 - mine) if (mask >> bit) & 1 else mine) * (1 << bit)
+        return total
+
+    masks = tuple(range(chips - 1, 0, -1))
+    others = [other(mask) for mask in masks]
+
+    def remote(src, dst, send, recv, target):
+        return pltpu.make_async_remote_copy(
+            src_ref=src, dst_ref=dst, send_sem=send, recv_sem=recv, device_id=(rep, target), device_id_type=MESH
+        )
+
+    def columns(owner, head):
+        return pl.ds(pl.multiple_of(owner * group_width + head * HEAD_DIM, HEAD_DIM), HEAD_DIM)
+
+    barrier = pltpu.get_barrier_semaphore()
+    pl.semaphore_signal(barrier, inc=1, device_id=(rep, partner), device_id_type=MESH)
+    for dest in others:
+        for side in range(CORES):
+            pl.semaphore_signal(barrier, inc=1, device_id=(rep, CORES * dest + side), device_id_type=MESH)
+    pl.semaphore_wait(barrier, CORES * chips - 1)
+
+    my_rows = pl.ds(pl.multiple_of(chip * rows, rows), rows)
+    my_toks = pl.ds(pl.multiple_of(me * toks, toks), toks)
+
+    def send_head(head, carry):
+        for dest in others:
+            cols = columns(dest, head)
+            remote(k_ref.at[:, cols], kv.at[head, 0, my_rows], kv_send, kv_recv.at[head], CORES * dest + core).start()
+            remote(v_ref.at[:, cols], kv.at[head, 1, my_rows], kv_send, kv_recv.at[head], CORES * dest + core).start()
+            for side in range(CORES):
+                remote(q_ref.at[side, :, cols], qs.at[head, my_toks], q_send, q_recv.at[head], CORES * dest + side).start()
+        cols = columns(chip, head)
+        pltpu.make_async_copy(k_ref.at[:, cols], kv.at[head, 0, my_rows], kv_recv.at[head]).start()
+        pltpu.make_async_copy(v_ref.at[:, cols], kv.at[head, 1, my_rows], kv_recv.at[head]).start()
+        pltpu.make_async_copy(q_ref.at[core, :, cols], qs.at[head, my_toks], q_recv.at[head]).start()
+        remote(q_ref.at[1 - core, :, cols], qs.at[head, my_toks], q_send, q_recv.at[head], partner).start()
+        return carry
+
+    lax.fori_loop(0, heads, send_head, 0)
+
+    def attend(head, carry):
+        direct = kv.at[head, :, pl.ds(0, half)]
+        passed = kv.at[head, :, pl.ds(half, half)]
+        pltpu.make_async_copy(direct, direct, kv_recv.at[head]).wait()
+        forward = remote(direct, passed, fwd_send.at[head], fwd_recv.at[head], partner)
+        forward.start()
+        pltpu.make_async_copy(qs.at[head], qs.at[head], q_recv.at[head]).wait()
+        forward.wait()
+        for start in range(0, qs.shape[1], ROW_CHUNK):
+            scores = lax.dot_general(
+                qs[head, start:start + ROW_CHUNK], kv[head, 0], (((1,), (1,)), ((), ())),
+                preferred_element_type=jnp.float32,
+            )
+            peak = jnp.max(scores, axis=1, keepdims=True)
+            expo = jnp.exp((scores - peak) * scale)
+            total = jnp.sum(expo, axis=1, keepdims=True)
+            summed = jnp.dot(expo.astype(jnp.bfloat16), kv[head, 1], preferred_element_type=jnp.float32)
+            res[head, start:start + ROW_CHUNK] = (summed / total).astype(jnp.bfloat16)
+        cols = columns(chip, head)
+
+        def block(device):
+            return res.at[head, pl.ds(pl.multiple_of(device * toks, toks), toks)]
+
+        place = out_ref.at[core, :, cols]
+        for dest in others:
+            for side in range(CORES):
+                device = CORES * dest + side
+                remote(block(device), place, o_send, o_recv, device).start()
+        remote(block(partner), place, o_send, o_recv, partner).start()
+        pltpu.make_async_copy(block(me), place, o_recv).start()
+        return carry
+
+    lax.fori_loop(0, heads, attend, 0)
+
+    pltpu.make_async_copy(out_ref, out_ref, o_recv).wait()
+    both = kv.at[:, :, pl.ds(0, (chips - 1) * rows)]
+    pltpu.make_async_copy(both, both, kv_send).wait()
+    most = qs.at[:, pl.ds(0, (CORES * chips - 1) * toks)]
+    pltpu.make_async_copy(most, most, q_send).wait()
+    pltpu.make_async_copy(most, most, o_send).wait()
+
+
+def by_heads(keys, values, queries):
+    nseq = lax.axis_size("seq")
+    chips = nseq // CORES
+    rows, width = keys.shape
+    _, toks, _ = queries.shape
+    heads = width // HEAD_DIM // chips
+    any_space = pl.BlockSpec(memory_space=pl.ANY)
+    dma = pltpu.SemaphoreType.DMA
+    return pl.pallas_call(
+        functools.partial(attend_kernel, chips, heads),
+        out_shape=jax.ShapeDtypeStruct(queries.shape, jnp.bfloat16),
+        in_specs=[any_space] * 3,
+        out_specs=any_space,
+        scratch_shapes=[
+            pltpu.VMEM((heads, 2, nseq * rows, HEAD_DIM), jnp.bfloat16),
+            pltpu.VMEM((heads, nseq * toks, HEAD_DIM), jnp.bfloat16),
+            pltpu.VMEM((heads, nseq * toks, HEAD_DIM), jnp.bfloat16),
+            dma, dma((heads,)), dma, dma((heads,)),
+            dma((heads,)), dma((heads,)), dma, dma,
+        ],
+        compiler_params=pltpu.CompilerParams(collective_id=0, has_side_effects=True),
+    )(keys, values, queries)
+
+
+def by_groups(keys, values, queries):
     nseq = lax.axis_size("seq")
     blocks = nseq // GROUPS
     ctx_rows, width = keys.shape
@@ -87,6 +216,15 @@
     return jnp.stack(layer_outs)
 
 
+def local(keys, values, queries):
+    chips = lax.axis_size("seq") // CORES
+    heads = keys.shape[1] // HEAD_DIM
+    whole_heads = heads % chips == 0 and chips & (chips - 1) == 0
+    if whole_heads and queries.shape[0] == CORES and queries.shape[1] % 16 == 0:
+        return by_heads(keys, values, queries)
+    return by_groups(keys, values, queries)
+
+
 def solution(mesh):
     return jax.shard_map(
         local,

time: 215 us -> 66.4 us (0.31); the launches traced: 212 us -> 66.3 us
  waiting for transfers between devices: 111 us -> 0 us
  Pallas kernels: 0 us -> 64.3 us
  starting transfers between devices: 52.2 us -> 0 us
  local copies, waits for them, and re-layouts: 22.8 us -> 1.97 us
  matrix products: 11.3 us -> 0 us
  other arithmetic: 6.99 us -> 0 us
  loops' own time: 6.76 us -> 0 us
    all_to_all x10 -> x0, waiting for transfers between devices: 111 us -> none  [the longest x2 48.3 us: local(): lax.all_to_all(shaped[0], 'seq', split_axis=1, concat_axis=1, tiled=True)]
    pallas_call x0 -> x1, Pallas kernels: none -> 64.3 us  [by_heads(): pl.pallas_call(functools.partial(attend_kernel, chips, heads), out_shape=...]
    all_to_all x10 -> x0, starting transfers between devices: 52.2 us -> none  [the longest x2 12 us: local(): lax.all_to_all(shaped[1], 'seq', split_axis=1, concat_axis=1, tiled=True)]
    dot_general x20 -> x0, matrix products: 11.3 us -> none  [the longest x10 7.66 us: one_head(): lax.dot_general(q_head, k_head, (((1,), (1,)), ((), ())), preferred_eleme...]
    reshape x14 -> x0, local copies, waits for them, and re-layouts: 7.66 us -> none  [the longest x2 3.66 us: local(): summed.reshape(heads_group, nseq, tok_rows, HEAD_DIM)]
    another operation x2 -> x0, loops' own time: 6.76 us -> none  [local(): lax.map(one_head, jnp.arange(heads_group, dtype=jnp.int32))]
    dynamic_slice x10 -> x0, local copies, waits for them, and re-layouts: 6.08 us -> none  [local(): lax.map(one_head, jnp.arange(heads_group, dtype=jnp.int32))]
    reduce_sum x14 -> x0, other arithmetic: 2.84 us -> none  [the longest x10 1.96 us: one_head(): total = jnp.sum(expo, axis=1)]
  transfers between devices with their start and end apart: 10 -> 0, of which waited for: 8 -> 0; matrix products, arithmetic and copies ran while one was open for 16% -> 0% of each run, Pallas kernels for 0% -> 0%
where the time goes in v1:
time: 66.4 us; the launch traced here: 66.3 us
  Pallas kernels  64.3 us (97%)
  local copies, waits for them, and re-layouts  1.97 us (3%)
    pallas_call x1, Pallas kernels, by_heads(): pl.pallas_call(functools.partial(attend_kernel, chips, heads), out_shape=...  64.3 us
    unnamed x1, local copies, waits for them, and re-layouts  1.97 us

profile of v1, /device:TPU:0, one launch (start us, length us, event | category | flops | bytes accessed | tf_op | source)
XLA Modules:
  0.0 66.3 jit_solution(7109127471971705086)
XLA Ops:
  0.0 64.3 %shard_map.37 = bf16[2,32,5120]{2,1,0:T(8,128)(2,1)} custom-call(bf16[64,5120]{1,0:T(8,128)(2,1)} %k_ref.1, bf16[64,5120]{1,0:T(8,128)(2,1)} %v_ref.1, bf16[2,32,5120]{2,1,0:T(8,128)(2,1)} %q_ref.1), custom_call_target="tpu_custom_call" | custom-call | tf_op jit(solution)/shard_map/pallas_call | solution.py:125
  64.3 2.0 %copy.5 = bf16[2,32,5120]{2,1,0:T(8,128)(2,1)} copy(bf16[2,32,5120]{2,1,0:T(8,128)(2,1)} %shard_map.37) | data formatting | bytes 1310720

commit v2 on v1

--- a/solution.py
+++ b/solution.py
@@ -56,21 +56,38 @@
     my_rows = pl.ds(pl.multiple_of(chip * rows, rows), rows)
     my_toks = pl.ds(pl.multiple_of(me * toks, toks), toks)
 
-    def send_head(head, carry):
-        for dest in others:
-            cols = columns(dest, head)
-            remote(k_ref.at[:, cols], kv.at[head, 0, my_rows], kv_send, kv_recv.at[head], CORES * dest + core).start()
-            remote(v_ref.at[:, cols], kv.at[head, 1, my_rows], kv_send, kv_recv.at[head], CORES * dest + core).start()
-            for side in range(CORES):
-                remote(q_ref.at[side, :, cols], qs.at[head, my_toks], q_send, q_recv.at[head], CORES * dest + side).start()
+    far = [other(mask) for mask in masks if mask >= 4]
+    close = [other(mask) for mask in masks if mask < 4]
+
+    def send_to(dest, head):
+        cols = columns(dest, head)
+        remote(k_ref.at[:, cols], kv.at[head, 0, my_rows], kv_send, kv_recv.at[head], CORES * dest + core).start()
+        remote(v_ref.at[:, cols], kv.at[head, 1, my_rows], kv_send, kv_recv.at[head], CORES * dest + core).start()
+        for side in range(CORES):
+            remote(q_ref.at[side, :, cols], qs.at[head, my_toks], q_send, q_recv.at[head], CORES * dest + side).start()
+
+    def keep(head):
         cols = columns(chip, head)
         pltpu.make_async_copy(k_ref.at[:, cols], kv.at[head, 0, my_rows], kv_recv.at[head]).start()
         pltpu.make_async_copy(v_ref.at[:, cols], kv.at[head, 1, my_rows], kv_recv.at[head]).start()
         pltpu.make_async_copy(q_ref.at[core, :, cols], qs.at[head, my_toks], q_recv.at[head]).start()
         remote(q_ref.at[1 - core, :, cols], qs.at[head, my_toks], q_send, q_recv.at[head], partner).start()
+
+    def send_all(dests):
+        def send_head(head, carry):
+            for dest in dests:
+                send_to(dest, head)
+            return carry
+
+        lax.fori_loop(0, heads, send_head, 0)
+
+    def keep_head(head, carry):
+        keep(head)
         return carry
 
-    lax.fori_loop(0, heads, send_head, 0)
+    send_all(far)
+    send_all(close)
+    lax.fori_loop(0, heads, keep_head, 0)
 
     def attend(head, carry):
         direct = kv.at[head, :, pl.ds(0, half)]
@@ -124,9 +141,9 @@
     dma = pltpu.SemaphoreType.DMA
     return pl.pallas_call(
         functools.partial(attend_kernel, chips, heads),
-        out_shape=jax.ShapeDtypeStruct(queries.shape, jnp.bfloat16),
+        out_shape=pltpu.VMEM(queries.shape, jnp.bfloat16),
         in_specs=[any_space] * 3,
-        out_specs=any_space,
+        out_specs=pl.BlockSpec(memory_space=pltpu.VMEM),
         scratch_shapes=[
             pltpu.VMEM((heads, 2, nseq * rows, HEAD_DIM), jnp.bfloat16),
             pltpu.VMEM((heads, nseq * toks, HEAD_DIM), jnp.bfloat16),
@@ -219,8 +236,7 @@
 def local(keys, values, queries):
     chips = lax.axis_size("seq") // CORES
     heads = keys.shape[1] // HEAD_DIM
-    whole_heads = heads % chips == 0 and chips & (chips - 1) == 0
-    if whole_heads and queries.shape[0] == CORES and queries.shape[1] % 16 == 0:
+    if chips == 8 and heads % chips == 0 and queries.shape[0] == CORES and queries.shape[1] % 16 == 0:
         return by_heads(keys, values, queries)
     return by_groups(keys, values, queries)
 

time: 66.4 us -> 65.1 us (0.980)
  local copies, waits for them, and re-layouts: 1.97 us -> 0.84 us
    unnamed x1, local copies, waits for them, and re-layouts: 1.97 us -> 0.84 us
where the time goes in v2:
time: 65.1 us; the launch traced here: 64.9 us
  Pallas kernels  64.1 us (98%)
  local copies, waits for them, and re-layouts  0.84 us (1%)
    pallas_call x1, Pallas kernels, by_heads(): pl.pallas_call(functools.partial(attend_kernel, chips, heads), out_shape=...  64.1 us

profile of v2, /device:TPU:0, one launch (start us, length us, event | category | flops | bytes accessed | tf_op | source)
XLA Modules:
  0.0 64.9 jit_solution(9528956096487671783)
XLA Ops:
  0.0 64.1 %shard_map.37 = bf16[2,32,5120]{2,1,0:T(8,128)(2,1)S(1)} custom-call(bf16[64,5120]{1,0:T(8,128)(2,1)} %k_ref.1, bf16[64,5120]{1,0:T(8,128)(2,1)} %v_ref.1, bf16[2,32,5120]{2,1,0:T(8,128)(2,1)} %q_ref.1), custom_call_target="tpu_custom_call" | custom-call | tf_op jit(solution)/shard_map/pallas_call | solution.py:142
  64.1 0.8 %copy.5 = bf16[2,32,5120]{2,1,0:T(8,128)(2,1)} copy(bf16[2,32,5120]{2,1,0:T(8,128)(2,1)S(1)} %shard_map.37) | data formatting | bytes 1310720

commit v3 on v2

--- a/solution.py
+++ b/solution.py
@@ -12,7 +12,6 @@
 GROUPS = 8
 CORES = 2
 MESH = pl.DeviceIdType.MESH
-ROW_CHUNK = 128
 
 
 def attend_kernel(chips, heads, k_ref, v_ref, q_ref, out_ref, kv, qs, res, kv_send, kv_recv, q_send, q_recv,
@@ -97,26 +96,27 @@
         forward.start()
         pltpu.make_async_copy(qs.at[head], qs.at[head], q_recv.at[head]).wait()
         forward.wait()
-        for start in range(0, qs.shape[1], ROW_CHUNK):
+        place = out_ref.at[core, :, columns(chip, head)]
+        chunk = 2 * CORES * toks
+
+        def block(device):
+            return res.at[head, pl.ds(pl.multiple_of(device * toks, toks), toks)]
+
+        for pair in range(chips // 2 - 1, -1, -1):
+            part = pl.ds(pl.multiple_of(lax.div(other(2 * pair), 2) * chunk, chunk), chunk)
             scores = lax.dot_general(
-                qs[head, start:start + ROW_CHUNK], kv[head, 0], (((1,), (1,)), ((), ())),
-                preferred_element_type=jnp.float32,
+                qs[head, part], kv[head, 0], (((1,), (1,)), ((), ())), preferred_element_type=jnp.float32
             )
             peak = jnp.max(scores, axis=1, keepdims=True)
             expo = jnp.exp((scores - peak) * scale)
             total = jnp.sum(expo, axis=1, keepdims=True)
             summed = jnp.dot(expo.astype(jnp.bfloat16), kv[head, 1], preferred_element_type=jnp.float32)
-            res[head, start:start + ROW_CHUNK] = (summed / total).astype(jnp.bfloat16)
-        cols = columns(chip, head)
-
-        def block(device):
-            return res.at[head, pl.ds(pl.multiple_of(device * toks, toks), toks)]
-
-        place = out_ref.at[core, :, cols]
-        for dest in others:
-            for side in range(CORES):
-                device = CORES * dest + side
-                remote(block(device), place, o_send, o_recv, device).start()
+            res[head, part] = (summed / total).astype(jnp.bfloat16)
+            for mask in (2 * pair, 2 * pair + 1):
+                if mask:
+                    for side in range(CORES):
+                        device = CORES * other(mask) + side
+                        remote(block(device), place, o_send, o_recv, device).start()
         remote(block(partner), place, o_send, o_recv, partner).start()
         pltpu.make_async_copy(block(me), place, o_recv).start()
         return carry

time: 65.1 us -> 65 us (level)
  no operation moved by 1% of the time
where the time goes in v3:
time: 65 us; the launch traced here: 64.9 us
  Pallas kernels  64 us (98%)
  local copies, waits for them, and re-layouts  0.84 us (1%)
    pallas_call x1, Pallas kernels, by_heads(): pl.pallas_call(functools.partial(attend_kernel, chips, heads), out_shape=...  64 us

profile of v3, /device:TPU:0, one launch (start us, length us, event | category | flops | bytes accessed | tf_op | source)
XLA Modules:
  0.0 64.9 jit_solution(4633000917900344095)
XLA Ops:
  0.0 64.0 %shard_map.37 = bf16[2,32,5120]{2,1,0:T(8,128)(2,1)S(1)} custom-call(bf16[64,5120]{1,0:T(8,128)(2,1)} %k_ref.1, bf16[64,5120]{1,0:T(8,128)(2,1)} %v_ref.1, bf16[2,32,5120]{2,1,0:T(8,128)(2,1)} %q_ref.1), custom_call_target="tpu_custom_call" | custom-call | tf_op jit(solution)/shard_map/pallas_call | solution.py:142
  64.0 0.8 %copy.5 = bf16[2,32,5120]{2,1,0:T(8,128)(2,1)} copy(bf16[2,32,5120]{2,1,0:T(8,128)(2,1)S(1)} %shard_map.37) | data formatting | bytes 1310720
